TPU v7x, 32 devices: a whole 2x2x4 slice. The times are simulated.
32 devices in a mesh: view: 2 (over y), tile: 16 (over z, x, core).
Axes of the slice: x: 2, y: 2, z: 4, core: 2. Of those that a mesh axis runs over, the one named last changes fastest.
Arguments:
- estimate: float32 [8, 512, 512], P(None, 'tile'), may hold values from 0.5 to 2
- observed: float32 [2, 8, 512, 512], P('view', None, 'tile'), may hold values from 0.2 to 4
- psf_taps: float32 [2, 3, 31], P('view'), may hold values from 0.05 to 1
Outputs:
- restored: float32 [8, 512, 512], P(None, 'tile')
All inputs are finite; a program needn't handle non-finite values.
Results may differ from a plain program's by a relative error of at most 0.0001.
Values sent between devices are 32-bit elements; how exact they have to be, the bound alone decides.
No kernel may reach another device: no remote copies, remote signals or barrier semaphores. Data moves between devices by JAX's collectives and lax.ppermute only.
A program may use at most 64 MiB of HBM per device.

v0:
```python
import jax
import jax.numpy as jnp
from jax import lax
from jax.sharding import PartitionSpec as P

ITERS = 2


def extended_2(cells, sides, width):
    for axis, dim in sides:
        count = lax.axis_size(axis)
        ends = count - 1
        head = lax.slice_in_dim(cells, 0, width, axis=dim)
        tail = lax.slice_in_dim(cells, cells.shape[dim] - width, cells.shape[dim], axis=dim)
        cells = jnp.concatenate(
            [
                lax.ppermute(tail, axis, [(i, (i + 1) % count) for i in range(ends)]),
                cells,
                lax.ppermute(head, axis, [((i + 1) % count, i) for i in range(ends)]),
            ],
            axis=dim,
        )
    return cells


def band_matrix(taps, count_in, count_out, offset):
    rows_in = jnp.arange(count_in)[:, None]
    cols_out = jnp.arange(count_out)[None, :]
    lag = rows_in - cols_out + offset
    length = taps.shape[0]
    inside = (lag >= 0) & (lag < length)
    return jnp.where(inside, jnp.take(taps, jnp.clip(lag, 0, length - 1)), 0.0)


def many_bands(taps, count_in, count_out, offset):
    return jax.vmap(lambda one: band_matrix(one, count_in, count_out, offset))(taps)


def blur(field, z_mats, y_mats, x_taps, cols_out):
    highest = lax.Precision.HIGHEST
    if field.ndim == 3:
        out = jnp.einsum("kyx,vkz->vzyx", field, z_mats, precision=highest)
    else:
        out = jnp.einsum("vkyx,vkz->vzyx", field, z_mats, precision=highest)
    out = jnp.einsum("vzjx,vjy->vzyx", out, y_mats, precision=highest)
    reach = (x_taps.shape[1] - 1) // 2
    pieces = []
    for start in range(0, cols_out, 128):
        block = min(128, cols_out - start)
        x_mats = many_bands(x_taps, block + 2 * reach, block, 0)
        piece = lax.slice_in_dim(out, start, start + block + 2 * reach, axis=3)
        pieces.append(jnp.einsum("vzyj,vjx->vzyx", piece, x_mats, precision=highest))
    return jnp.concatenate(pieces, axis=3)


def body(estimate, observed, psf_taps):
    depth, rows, width = estimate.shape
    half = (psf_taps.shape[2] - 1) // 2
    views = lax.axis_size("view")
    recorded = lax.all_to_all(observed, "view", split_axis=3, concat_axis=0, tiled=True)
    taps = lax.all_gather(psf_taps, "view", axis=0, tiled=True)
    cols = width // views
    col_start = lax.axis_index("view") * cols
    current = lax.dynamic_slice_in_dim(estimate, col_start, cols, 2)
    normed = taps / jnp.sum(taps, axis=2, keepdims=True)
    flipped = normed[:, :, ::-1]
    fwd_z = many_bands(normed[:, 0], depth, depth, half)
    back_z = many_bands(flipped[:, 0], depth, depth, half)
    back_y = many_bands(flipped[:, 1], rows + 2 * half, rows, 0)
    fwd_y = many_bands(normed[:, 1], rows + 2 * half, rows, 0)
    for step in range(ITERS):
        extended = extended_2(current, (("view", 2), ("tile", 1)), half)
        blurred = blur(extended, fwd_z, fwd_y, normed[:, 2], cols)
        ratio = recorded / blurred
        ratio_ext = extended_2(ratio, (("view", 3), ("tile", 2)), half)
        log_corr = jnp.log(blur(ratio_ext, back_z, back_y, flipped[:, 2], cols))
        log_total = jnp.sum(log_corr, axis=0)
        current = current * jnp.exp(log_total / views)
    current = lax.all_gather(current, "view", axis=2, tiled=True)
    return current


def solution(mesh):
    placed = (P(None, "tile", None), P("view", None, "tile", None), P("view", None, None))
    return jax.shard_map(
        body, mesh=mesh, in_specs=placed, out_specs=P(None, "tile", None), check_vma=False
    )
```

profile of v0, /device:TPU:19, one launch (start us, length us, event | category | flops | bytes accessed | tf_op | source)
XLA Modules:
  0.0 232.7 jit_solution(4656722165472639557)
XLA Ops:
  2.0 3.8 %collective-permute-start = (f32[8,32,15]{2,0,1:T(8,128)}, f32[8,32,15]{2,0,1:T(8,128)}, u32[]{:S(2)}, u32[]{:S(2)}) collective-permute-start(f32[8,32,15]{2,0,1:T(8,128)} %get-tuple-element.22), channel_id=1, source_target_pairs={{0,16},{1,17},{2,18},{3,19},{4,20},{5,21},{6,22},{7,23},{8,24},{9,... | collective-permute-start | bytes 46088 | tf_op jit(solution)/shard_map/ppermute | solution.py:17
  9.5 4.0 %all-to-all-start = ((f32[2,1,65536]{2,1,0:T(1,128)}), f32[2,1,65536]{2,1,0:T(1,128)S(1)}, u32[]{:S(2)}, u32[]{:S(2)}) async-start(f32[2,1,65536]{2,1,0:T(1,128)} %reshape.110), calls=%async_computation | async-start | bytes 1048576 | tf_op jit(solution)/shard_map/all_to_all | solution.py:60
  13.6 7.8 %all_gather.6 = f32[2,3,31]{2,1,0:T(4,128)S(1)} all-gather(f32[1,3,31]{2,1,0:T(4,128)S(1)} %copy.97), channel_id=1, replica_groups=mesh['view'=2,'tile'=16] {'view'}, dimensions={0}, use_global_device_ids=true | all-gather | bytes 1116 | tf_op jit(solution)/shard_map/all_gather | solution.py:61
  23.1 5.0 %collective-permute-start.2 = (f32[8,15,286]{2,0,1:T(8,128)S(1)}, f32[8,15,286]{2,0,1:T(8,128)S(1)}, u32[]{:S(2)}, u32[]{:S(2)}) collective-permute-start(f32[8,15,286]{2,0,1:T(8,128)S(1)} %get-tuple-element.18), channel_id=1, source_target_pairs={{0,1},{1,2},{2,3},{3,4},{4,5},{5,6},{6,7},{7,8},{8,9},{9,10},{10,1... | collective-permute-start | bytes 411848 | tf_op jit(solution)/shard_map/ppermute | solution.py:17
  31.0 5.6 %gather_fusion.2 = f32[1984,2]{1,0:T(8,128)S(1)} fusion(f32[2,31]{0,1:T(8,128)S(1)} %copy.107, s32[2048]{0:T(1024)S(1)} %pad_clamp_fusion.1), kind=kCustom, calls=%fused_computation.3.clone | custom fusion | bytes 39680 | tf_op jit(solution)/shard_map/vmap(jit(_take))/gather | solution.py:32
  37.2 37.8 %gather_fusion.4 = f32[20224,2]{1,0:T(8,128)} fusion(f32[2,31]{0,1:T(8,128)S(1)} %copy.113, s32[20480]{0:T(1024)S(1)} %pad_clamp_fusion), kind=kCustom, calls=%fused_computation.2.clone | custom fusion | bytes 404480 | tf_op jit(solution)/shard_map/vmap(jit(_take))/gather | solution.py:32
  75.0 6.0 %copy.114 = f32[158,128,2]{1,0,2:T(8,128)S(1)} copy(f32[158,128,2]{2,1,0:T(8,128)} %bitcast.150) | data formatting | bytes 323584 | tf_op jit(solution)/shard_map/vmap(jit(_take))/gather | solution.py:32
  81.1 2.5 %fusion.24 = f32[2,8,62,286]{3,1,2,0:T(8,128)S(1)} fusion(f32[8,15,286]{2,0,1:T(8,128)} %collective-permute-done.3, f32[8,32,15]{2,0,1:T(8,128)} %collective-permute-done.1, f32[8,32,256]{2,0,1:T(8,128)S(1)} %copy.148, f32[8,32,15]{2,0,1:T(8,128)} %collective-permute-done, f32[8,15,286]{2,0,1:T(8,128)S(1)} %collective-permute-done.2, ...), kind=kOutput, calls=%fused_computation.27 | convolution fusion | flops 27804032 | bytes 1702912 | tf_op jit(solution)/shard_map/kyx,vkz->vzyx/dot_general | solution.py:42
  87.8 2.3 reduce
  95.7 3.8 %collective-permute-done.4 = f32[2,8,32,15]{3,2,1,0:T(8,128)S(1)} collective-permute-done((f32[2,8,32,15]{3,2,1,0:T(8,128)S(1)}, f32[2,8,32,15]{3,2,1,0:T(8,128)S(1)}, u32[]{:S(2)}, u32[]{:S(2)}) %collective-permute-start.4) | collective-permute-done | bytes 30752 | tf_op jit(solution)/shard_map/ppermute | solution.py:17
  99.4 3.8 %collective-permute-done.5 = f32[2,8,32,15]{3,2,1,0:T(8,128)S(1)} collective-permute-done((f32[2,8,32,15]{3,2,1,0:T(8,128)S(1)}, f32[2,8,32,15]{3,2,1,0:T(8,128)S(1)}, u32[]{:S(2)}, u32[]{:S(2)}) %collective-permute-start.5) | collective-permute-done | bytes 30752 | tf_op jit(solution)/shard_map/ppermute | solution.py:19
  104.6 4.7 %collective-permute-start.6 = (f32[2,8,15,286]{3,2,1,0:T(8,128)}, f32[2,8,15,286]{3,2,1,0:T(8,128)}, u32[]{:S(2)}, u32[]{:S(2)}) collective-permute-start(f32[2,8,15,286]{3,2,1,0:T(8,128)} %get-tuple-element.10), channel_id=1, source_target_pairs={{0,1},{1,2},{2,3},{3,4},{4,5},{5,6},{6,7},{7,8},{8,9},{9,10},{10,1... | collective-permute-start | bytes 823688 | tf_op jit(solution)/shard_map/ppermute | solution.py:17
  112.7 5.6 %gather_fusion = f32[1984,2]{1,0:T(8,128)S(1)} fusion(f32[2,31]{0,1:T(8,128)S(1)} %copy.99, s32[2048]{0:T(1024)S(1)} %pad_clamp_fusion.1), kind=kCustom, calls=%fused_computation.clone | custom fusion | bytes 39680 | tf_op jit(solution)/shard_map/vmap(jit(_take))/gather | solution.py:32
  118.9 37.8 %gather_fusion.5 = f32[20224,2]{1,0:T(8,128)} fusion(f32[2,31]{0,1:T(8,128)S(1)} %copy.118, s32[20480]{0:T(1024)S(1)} %pad_clamp_fusion), kind=kCustom, calls=%fused_computation.5.clone | custom fusion | bytes 404480 | tf_op jit(solution)/shard_map/vmap(jit(_take))/gather | solution.py:32
  156.7 6.0 %copy.119 = f32[158,128,2]{1,0,2:T(8,128)S(1)} copy(f32[158,128,2]{2,1,0:T(8,128)} %bitcast.149) | data formatting | bytes 323584 | tf_op jit(solution)/shard_map/vmap(jit(_take))/gather | solution.py:32
  172.9 3.8 %collective-permute-done.9 = f32[8,32,15]{2,0,1:T(8,128)S(1)} collective-permute-done((f32[8,32,15]{2,0,1:T(8,128)S(1)}, f32[8,32,15]{2,0,1:T(8,128)S(1)}, u32[]{:S(2)}, u32[]{:S(2)}) %collective-permute-start.9) | collective-permute-done | bytes 15392 | tf_op jit(solution)/shard_map/ppermute | solution.py:19
  177.0 5.4 %collective-permute-start.10 = (f32[8,15,286]{2,0,1:T(8,128)S(1)}, f32[8,15,286]{2,0,1:T(8,128)S(1)}, u32[]{:S(2)}, u32[]{:S(2)}) collective-permute-start(f32[8,15,286]{2,0,1:T(8,128)S(1)} %get-tuple-element.14), channel_id=1, source_target_pairs={{0,1},{1,2},{2,3},{3,4},{4,5},{5,6},{6,7},{7,8},{8,9},{9,10},{10,1... | collective-permute-start | bytes 411848 | tf_op jit(solution)/shard_map/ppermute | solution.py:17
  184.9 5.3 %collective-permute-done.11 = f32[8,15,286]{2,0,1:T(8,128)S(1)} collective-permute-done((f32[8,15,286]{2,0,1:T(8,128)S(1)}, f32[8,15,286]{2,0,1:T(8,128)S(1)}, u32[]{:S(2)}, u32[]{:S(2)}) %collective-permute-start.11) | collective-permute-done | bytes 137312 | tf_op jit(solution)/shard_map/ppermute | solution.py:19
  196.8 2.2 collective-permute-done.12
  199.0 4.1 %collective-permute-done.13 = f32[2,8,32,15]{3,2,1,0:T(8,128)S(1)} collective-permute-done((f32[2,8,32,15]{3,2,1,0:T(8,128)S(1)}, f32[2,8,32,15]{3,2,1,0:T(8,128)S(1)}, u32[]{:S(2)}, u32[]{:S(2)}) %collective-permute-start.13) | collective-permute-done | bytes 30752 | tf_op jit(solution)/shard_map/ppermute | solution.py:19
  203.5 4.3 %collective-permute-start.14 = (f32[2,8,15,286]{3,2,1,0:T(8,128)S(1)}, f32[2,8,15,286]{3,2,1,0:T(8,128)S(1)}, u32[]{:S(2)}, u32[]{:S(2)}) collective-permute-start(f32[2,8,15,286]{3,2,1,0:T(8,128)S(1)} %get-tuple-element.6), channel_id=1, source_target_pairs={{0,1},{1,2},{2,3},{3,4},{4,5},{5,6},{6,7},{7,8},{8,9},{9,10},{10,1... | collective-permute-start | bytes 823688 | tf_op jit(solution)/shard_map/ppermute | solution.py:17
  210.0 2.6 %collective-permute-done.14 = f32[2,8,15,286]{3,2,1,0:T(8,128)S(1)} collective-permute-done((f32[2,8,15,286]{3,2,1,0:T(8,128)S(1)}, f32[2,8,15,286]{3,2,1,0:T(8,128)S(1)}, u32[]{:S(2)}, u32[]{:S(2)}) %collective-permute-start.14) | collective-permute-done | bytes 274592 | tf_op jit(solution)/shard_map/ppermute | solution.py:17
  212.6 5.3 %collective-permute-done.15 = f32[2,8,15,286]{3,2,1,0:T(8,128)S(1)} collective-permute-done((f32[2,8,15,286]{3,2,1,0:T(8,128)S(1)}, f32[2,8,15,286]{3,2,1,0:T(8,128)S(1)}, u32[]{:S(2)}, u32[]{:S(2)}) %collective-permute-start.15) | collective-permute-done | bytes 274592 | tf_op jit(solution)/shard_map/ppermute | solution.py:19
  223.1 8.6 %all_gather.7 = f32[8,32,512]{2,0,1:T(8,128)S(1)} all-gather(f32[8,32,256]{2,0,1:T(8,128)S(1)} %fusion.61), channel_id=1, replica_groups=mesh['view'=2,'tile'=16] {'view'}, dimensions={2}, use_global_device_ids=true | all-gather | bytes 786432 | tf_op jit(solution)/shard_map/all_gather | solution.py:79
  (102 shorter events, 54.3 us)
Async XLA Ops:
  0.0 1.0 copy-start
  0.0 7.1 %copy-start.3 = (f32[1,8,32,512]{3,2,1,0:T(8,128)S(1)}, f32[1,8,32,512]{3,2,1,0:T(8,128)}, u32[]{:S(2)}) copy-start(f32[1,8,32,512]{3,2,1,0:T(8,128)} %param.10) | copy-start | bytes 1572868
  1.1 4.7 %copy-start.1 = (f32[8,32,256]{2,1,0:T(8,128)}, f32[8,32,256]{2,1,0:T(8,128)S(1)}, u32[]{:S(2)}) copy-start(f32[8,32,256]{2,1,0:T(8,128)S(1)} %constant_dynamic-slice_fusion) | copy-start | bytes 786436
  2.0 19.9 %collective-permute-start = (f32[8,32,15]{2,0,1:T(8,128)}, f32[8,32,15]{2,0,1:T(8,128)}, u32[]{:S(2)}, u32[]{:S(2)}) collective-permute-start(f32[8,32,15]{2,0,1:T(8,128)} %get-tuple-element.22), channel_id=1, source_target_pairs={{0,16},{1,17},{2,18},{3,19},{4,20},{5,21},{6,22},{7,23},{8,24},{9,... | collective-permute-start | bytes 46088 | tf_op jit(solution)/shard_map/ppermute | solution.py:17
  5.8 16.1 %collective-permute-start.1 = (f32[8,32,15]{2,0,1:T(8,128)}, f32[8,32,15]{2,0,1:T(8,128)}, u32[]{:S(2)}, u32[]{:S(2)}) collective-permute-start(f32[8,32,15]{2,0,1:T(8,128)} %get-tuple-element.23), channel_id=1, source_target_pairs={{16,0},{17,1},{18,2},{19,3},{20,4},{21,5},{22,6},{23,7},{24,8},{25... | collective-permute-start | bytes 46088 | tf_op jit(solution)/shard_map/ppermute | solution.py:19
  7.9 5.7 %copy-start.4 = (f32[1,3,31]{2,0,1:T(1,128)S(1)}, f32[1,3,31]{2,0,1:T(1,128)}, u32[]{:S(2)}) copy-start(f32[1,3,31]{2,0,1:T(1,128)} %param.11) | copy-start | bytes 1120
  9.5 77.8 %all-to-all-start = ((f32[2,1,65536]{2,1,0:T(1,128)}), f32[2,1,65536]{2,1,0:T(1,128)S(1)}, u32[]{:S(2)}, u32[]{:S(2)}) async-start(f32[2,1,65536]{2,1,0:T(1,128)} %reshape.110), calls=%async_computation | async-start | bytes 1048576 | tf_op jit(solution)/shard_map/all_to_all | solution.py:60
  23.1 58.0 %collective-permute-start.2 = (f32[8,15,286]{2,0,1:T(8,128)S(1)}, f32[8,15,286]{2,0,1:T(8,128)S(1)}, u32[]{:S(2)}, u32[]{:S(2)}) collective-permute-start(f32[8,15,286]{2,0,1:T(8,128)S(1)} %get-tuple-element.18), channel_id=1, source_target_pairs={{0,1},{1,2},{2,3},{3,4},{4,5},{5,6},{6,7},{7,8},{8,9},{9,10},{10,1... | collective-permute-start | bytes 411848 | tf_op jit(solution)/shard_map/ppermute | solution.py:17
  28.0 53.1 %collective-permute-start.3 = (f32[8,15,286]{2,0,1:T(8,128)S(1)}, f32[8,15,286]{2,0,1:T(8,128)}, u32[]{:S(2)}, u32[]{:S(2)}) collective-permute-start(f32[8,15,286]{2,0,1:T(8,128)S(1)} %get-tuple-element.19), channel_id=1, source_target_pairs={{1,0},{2,1},{3,2},{4,3},{5,4},{6,5},{7,6},{8,7},{9,8},{10,9},{11,1... | collective-permute-start | bytes 411848 | tf_op jit(solution)/shard_map/ppermute | solution.py:19
  92.9 6.5 %collective-permute-start.4 = (f32[2,8,32,15]{3,2,1,0:T(8,128)S(1)}, f32[2,8,32,15]{3,2,1,0:T(8,128)S(1)}, u32[]{:S(2)}, u32[]{:S(2)}) collective-permute-start(f32[2,8,32,15]{3,2,1,0:T(8,128)S(1)} %get-tuple-element.16), channel_id=1, source_target_pairs={{0,16},{1,17},{2,18},{3,19},{4,20},{5,21},{6,22},{7,23},{8,24},{9,... | collective-permute-start | bytes 92168 | tf_op jit(solution)/shard_map/ppermute | solution.py:17
  94.4 8.9 %collective-permute-start.5 = (f32[2,8,32,15]{3,2,1,0:T(8,128)S(1)}, f32[2,8,32,15]{3,2,1,0:T(8,128)S(1)}, u32[]{:S(2)}, u32[]{:S(2)}) collective-permute-start(f32[2,8,32,15]{3,2,1,0:T(8,128)S(1)} %get-tuple-element.17), channel_id=1, source_target_pairs={{16,0},{17,1},{18,2},{19,3},{20,4},{21,5},{22,6},{23,7},{24,8},{25... | collective-permute-start | bytes 92168 | tf_op jit(solution)/shard_map/ppermute | solution.py:19
  104.6 58.2 %collective-permute-start.6 = (f32[2,8,15,286]{3,2,1,0:T(8,128)}, f32[2,8,15,286]{3,2,1,0:T(8,128)}, u32[]{:S(2)}, u32[]{:S(2)}) collective-permute-start(f32[2,8,15,286]{3,2,1,0:T(8,128)} %get-tuple-element.10), channel_id=1, source_target_pairs={{0,1},{1,2},{2,3},{3,4},{4,5},{5,6},{6,7},{7,8},{8,9},{9,10},{10,1... | collective-permute-start | bytes 823688 | tf_op jit(solution)/shard_map/ppermute | solution.py:17
  109.3 53.4 %collective-permute-start.7 = (f32[2,8,15,286]{3,2,1,0:T(8,128)}, f32[2,8,15,286]{3,2,1,0:T(8,128)}, u32[]{:S(2)}, u32[]{:S(2)}) collective-permute-start(f32[2,8,15,286]{3,2,1,0:T(8,128)} %get-tuple-element.11), channel_id=1, source_target_pairs={{1,0},{2,1},{3,2},{4,3},{5,4},{6,5},{7,6},{8,7},{9,8},{10,9},{11,1... | collective-permute-start | bytes 823688 | tf_op jit(solution)/shard_map/ppermute | solution.py:19
  167.5 1.3 copy-start.2
  169.3 3.6 %collective-permute-start.8 = (f32[8,32,15]{2,0,1:T(8,128)S(1)}, f32[8,32,15]{2,0,1:T(8,128)S(1)}, u32[]{:S(2)}, u32[]{:S(2)}) collective-permute-start(f32[8,32,15]{2,0,1:T(8,128)S(1)} %get-tuple-element.20), channel_id=1, source_target_pairs={{0,16},{1,17},{2,18},{3,19},{4,20},{5,21},{6,22},{7,23},{8,24},{9,... | collective-permute-start | bytes 46088 | tf_op jit(solution)/shard_map/ppermute | solution.py:17
  170.6 6.2 %collective-permute-start.9 = (f32[8,32,15]{2,0,1:T(8,128)S(1)}, f32[8,32,15]{2,0,1:T(8,128)S(1)}, u32[]{:S(2)}, u32[]{:S(2)}) collective-permute-start(f32[8,32,15]{2,0,1:T(8,128)S(1)} %get-tuple-element.21), channel_id=1, source_target_pairs={{16,0},{17,1},{18,2},{19,3},{20,4},{21,5},{22,6},{23,7},{24,8},{25... | collective-permute-start | bytes 46088 | tf_op jit(solution)/shard_map/ppermute | solution.py:19
  177.0 7.9 %collective-permute-start.10 = (f32[8,15,286]{2,0,1:T(8,128)S(1)}, f32[8,15,286]{2,0,1:T(8,128)S(1)}, u32[]{:S(2)}, u32[]{:S(2)}) collective-permute-start(f32[8,15,286]{2,0,1:T(8,128)S(1)} %get-tuple-element.14), channel_id=1, source_target_pairs={{0,1},{1,2},{2,3},{3,4},{4,5},{5,6},{6,7},{7,8},{8,9},{9,10},{10,1... | collective-permute-start | bytes 411848 | tf_op jit(solution)/shard_map/ppermute | solution.py:17
  182.4 7.8 %collective-permute-start.11 = (f32[8,15,286]{2,0,1:T(8,128)S(1)}, f32[8,15,286]{2,0,1:T(8,128)S(1)}, u32[]{:S(2)}, u32[]{:S(2)}) collective-permute-start(f32[8,15,286]{2,0,1:T(8,128)S(1)} %get-tuple-element.15), channel_id=1, source_target_pairs={{1,0},{2,1},{3,2},{4,3},{5,4},{6,5},{7,6},{8,7},{9,8},{10,9},{11,1... | collective-permute-start | bytes 411848 | tf_op jit(solution)/shard_map/ppermute | solution.py:19
  194.2 4.8 %collective-permute-start.12 = (f32[2,8,32,15]{3,2,1,0:T(8,128)S(1)}, f32[2,8,32,15]{3,2,1,0:T(8,128)S(1)}, u32[]{:S(2)}, u32[]{:S(2)}) collective-permute-start(f32[2,8,32,15]{3,2,1,0:T(8,128)S(1)} %get-tuple-element.12), channel_id=1, source_target_pairs={{0,16},{1,17},{2,18},{3,19},{4,20},{5,21},{6,22},{7,23},{8,24},{9,... | collective-permute-start | bytes 92168 | tf_op jit(solution)/shard_map/ppermute | solution.py:17
  195.5 7.6 %collective-permute-start.13 = (f32[2,8,32,15]{3,2,1,0:T(8,128)S(1)}, f32[2,8,32,15]{3,2,1,0:T(8,128)S(1)}, u32[]{:S(2)}, u32[]{:S(2)}) collective-permute-start(f32[2,8,32,15]{3,2,1,0:T(8,128)S(1)} %get-tuple-element.13), channel_id=1, source_target_pairs={{16,0},{17,1},{18,2},{19,3},{20,4},{21,5},{22,6},{23,7},{24,8},{25... | collective-permute-start | bytes 92168 | tf_op jit(solution)/shard_map/ppermute | solution.py:19
  203.5 9.0 %collective-permute-start.14 = (f32[2,8,15,286]{3,2,1,0:T(8,128)S(1)}, f32[2,8,15,286]{3,2,1,0:T(8,128)S(1)}, u32[]{:S(2)}, u32[]{:S(2)}) collective-permute-start(f32[2,8,15,286]{3,2,1,0:T(8,128)S(1)} %get-tuple-element.6), channel_id=1, source_target_pairs={{0,1},{1,2},{2,3},{3,4},{4,5},{5,6},{6,7},{7,8},{8,9},{9,10},{10,1... | collective-permute-start | bytes 823688 | tf_op jit(solution)/shard_map/ppermute | solution.py:17
  207.8 10.0 %collective-permute-start.15 = (f32[2,8,15,286]{3,2,1,0:T(8,128)S(1)}, f32[2,8,15,286]{3,2,1,0:T(8,128)S(1)}, u32[]{:S(2)}, u32[]{:S(2)}) collective-permute-start(f32[2,8,15,286]{3,2,1,0:T(8,128)S(1)} %get-tuple-element.8), channel_id=1, source_target_pairs={{1,0},{2,1},{3,2},{4,3},{5,4},{6,5},{7,6},{8,7},{9,8},{10,9},{11,1... | collective-permute-start | bytes 823688 | tf_op jit(solution)/shard_map/ppermute | solution.py:19
where the time goes:
time: 233 us
  local copies, waits for them, and re-layouts  111 us (48%)
  starting transfers between devices  44.4 us (19%)
  waiting for transfers between devices  32.5 us (14%)
  matrix products  18.9 us (8%)
  blocking collectives  16.4 us (7%)
  other arithmetic  8.52 us (4%)
    gather x12, local copies, waits for them, and re-layouts, band_matrix(): return jnp.where(inside, jnp.take(taps, jnp.clip(lag, 0, length - 1)), 0.0)  101 us
    ppermute x8, starting transfers between devices, extended_2(): lax.ppermute(tail, axis, [(i, (i + 1) % count) for i in range(ends)])  27.2 us
    ppermute x8, waiting for transfers between devices, extended_2(): lax.ppermute(head, axis, [((i + 1) % count, i) for i in range(ends)])  22.4 us
    ppermute x8, starting transfers between devices, extended_2(): lax.ppermute(head, axis, [((i + 1) % count, i) for i in range(ends)])  13.2 us
    ppermute x8, waiting for transfers between devices, extended_2(): lax.ppermute(tail, axis, [(i, (i + 1) % count) for i in range(ends)])  10.1 us
    all_gather x1, blocking collectives, body(): current = lax.all_gather(current, 'view', axis=2, tiled=True)  8.58 us
    all_gather x1, blocking collectives, body(): taps = lax.all_gather(psf_taps, 'view', axis=0, tiled=True)  7.85 us
    dot_general x8, matrix products, blur(): jnp.einsum('vzyj,vjx->vzyx', piece, x_mats, precision=highest)  6.3 us
  transfers between devices with their start and end apart: 17, of which 10 were waited for; matrix products, arithmetic and copies ran while one was open for 48% of the time, Pallas kernels for 0%

commit v1 on v0

--- a/solution.py
+++ b/solution.py
@@ -2,8 +2,18 @@
 import jax.numpy as jnp
 from jax import lax
 from jax.sharding import PartitionSpec as P
+from jax.lax import all_to_all, axis_size
 
 ITERS = 2
+
+
+def _fill_terms(row_dim, dim_k, axis_tag, local):
+    k_now = axis_size(axis_tag)
+    part_now = jnp.split(local, k_now, row_dim)
+    piece_next = jnp.stack(part_now, 0)
+    n_now = all_to_all(piece_next, axis_tag, 0, 0)
+    y_new = jnp.concatenate(n_now, dim_k)
+    return y_new
 
 
 def extended_2(cells, sides, width):
@@ -57,7 +67,7 @@
     depth, rows, width = estimate.shape
     half = (psf_taps.shape[2] - 1) // 2
     views = lax.axis_size("view")
-    recorded = lax.all_to_all(observed, "view", split_axis=3, concat_axis=0, tiled=True)
+    recorded = _fill_terms(3, 0, axis_tag="view", local=observed)
     taps = lax.all_gather(psf_taps, "view", axis=0, tiled=True)
     cols = width // views
     col_start = lax.axis_index("view") * cols

time: 233 us -> 224 us (0.961)
  local copies, waits for them, and re-layouts: 111 us -> 108 us
  other arithmetic: 8.52 us -> 5.81 us
    unnamed x15 -> x28, local copies, waits for them, and re-layouts: 4.48 us -> 1.25 us
  transfers between devices with their start and end apart: 17 -> 17, of which waited for: 10 -> 10; matrix products, arithmetic and copies ran while one was open for 48% -> 49% of each run, Pallas kernels for 0% -> 0%
where the time goes in v1:
time: 224 us
  local copies, waits for them, and re-layouts  108 us (48%)
  starting transfers between devices  43.2 us (19%)
  waiting for transfers between devices  32.5 us (15%)
  matrix products  17.5 us (8%)
  blocking collectives  16.3 us (7%)
  other arithmetic  5.81 us (3%)
    gather x12, local copies, waits for them, and re-layouts, band_matrix(): return jnp.where(inside, jnp.take(taps, jnp.clip(lag, 0, length - 1)), 0.0)  103 us
    ppermute x8, starting transfers between devices, extended_2(): lax.ppermute(tail, axis, [(i, (i + 1) % count) for i in range(ends)])  26.5 us
    ppermute x8, waiting for transfers between devices, extended_2(): lax.ppermute(head, axis, [((i + 1) % count, i) for i in range(ends)])  22.4 us
    ppermute x8, starting transfers between devices, extended_2(): lax.ppermute(head, axis, [((i + 1) % count, i) for i in range(ends)])  13.3 us
    ppermute x8, waiting for transfers between devices, extended_2(): lax.ppermute(tail, axis, [(i, (i + 1) % count) for i in range(ends)])  10.1 us
    all_gather x1, blocking collectives, body(): current = lax.all_gather(current, 'view', axis=2, tiled=True)  8.59 us
    all_gather x1, blocking collectives, body(): taps = lax.all_gather(psf_taps, 'view', axis=0, tiled=True)  7.69 us
    dot_general x8, matrix products, blur(): jnp.einsum('vzyj,vjx->vzyx', piece, x_mats, precision=highest)  4.9 us
  transfers between devices with their start and end apart: 17, of which 10 were waited for; matrix products, arithmetic and copies ran while one was open for 49% of the time, Pallas kernels for 0%

profile of v1, /device:TPU:19, one launch (start us, length us, event | category | flops | bytes accessed | tf_op | source)
XLA Modules:
  0.0 223.7 jit_solution(18413798909415409846)
XLA Ops:
  1.3 3.2 %collective-permute-start = (f32[8,32,15]{2,0,1:T(8,128)S(1)}, f32[8,32,15]{2,0,1:T(8,128)S(1)}, u32[]{:S(2)}, u32[]{:S(2)}) collective-permute-start(f32[8,32,15]{2,0,1:T(8,128)S(1)} %get-tuple-element.24), channel_id=1, source_target_pairs={{0,16},{1,17},{2,18},{3,19},{4,20},{5,21},{6,22},{7,23},{8,24},{9,... | collective-permute-start | bytes 46088 | tf_op jit(solution)/shard_map/ppermute | solution.py:27
  6.7 3.5 %all-to-all-start = ((f32[2,1,8,32,256]{4,3,2,1,0:T(8,128)}), f32[2,1,8,32,256]{4,3,2,1,0:T(8,128)S(1)}, u32[]{:S(2)}, u32[]{:S(2)}) async-start(f32[2,1,8,32,256]{4,3,2,1,0:T(8,128)} %pad_maximum_fusion.4), calls=%async_computation | async-start | bytes 1048576 | tf_op jit(solution)/shard_map/all_to_all | solution.py:14
  10.3 7.7 %all_gather.6 = f32[2,3,31]{2,1,0:T(4,128)S(1)} all-gather(f32[1,3,31]{2,1,0:T(4,128)S(1)} %copy.90), channel_id=1, replica_groups=mesh['view'=2,'tile'=16] {'view'}, dimensions={0}, use_global_device_ids=true | all-gather | bytes 1116 | tf_op jit(solution)/shard_map/all_gather | solution.py:71
  19.4 4.9 %collective-permute-start.2 = (f32[8,15,286]{2,0,1:T(8,128)}, f32[8,15,286]{2,0,1:T(8,128)}, u32[]{:S(2)}, u32[]{:S(2)}) collective-permute-start(f32[8,15,286]{2,0,1:T(8,128)} %get-tuple-element.20), channel_id=1, source_target_pairs={{0,1},{1,2},{2,3},{3,4},{4,5},{5,6},{6,7},{7,8},{8,9},{9,10},{10,1... | collective-permute-start | bytes 411848 | tf_op jit(solution)/shard_map/ppermute | solution.py:27
  27.3 5.6 %gather_fusion.2 = f32[1984,2]{1,0:T(8,128)S(1)} fusion(f32[2,31]{0,1:T(8,128)S(1)} %copy.97, s32[2048]{0:T(1024)S(1)} %pad_clamp_fusion.1), kind=kCustom, calls=%fused_computation.3.clone | custom fusion | bytes 39680 | tf_op jit(solution)/shard_map/vmap(jit(_take))/gather | solution.py:42
  33.5 37.8 %gather_fusion.4 = f32[20224,2]{1,0:T(8,128)} fusion(f32[2,31]{0,1:T(8,128)S(1)} %copy.103, s32[20480]{0:T(1024)S(1)} %pad_clamp_fusion), kind=kCustom, calls=%fused_computation.2.clone | custom fusion | bytes 404480 | tf_op jit(solution)/shard_map/vmap(jit(_take))/gather | solution.py:42
  71.4 6.0 %copy.104 = f32[158,128,2]{1,0,2:T(8,128)S(1)} copy(f32[158,128,2]{2,1,0:T(8,128)} %bitcast.149) | data formatting | bytes 323584 | tf_op jit(solution)/shard_map/vmap(jit(_take))/gather | solution.py:42
  77.4 2.4 %fusion.24 = f32[2,8,62,286]{3,1,2,0:T(8,128)S(1)} fusion(f32[8,15,286]{2,0,1:T(8,128)} %collective-permute-done.3, f32[8,32,15]{2,0,1:T(8,128)S(1)} %collective-permute-done.1, f32[8,32,256]{2,0,1:T(8,128)S(1)} %copy.136, f32[8,32,15]{2,0,1:T(8,128)S(1)} %collective-permute-done, f32[8,15,286]{2,0,1:T(8,128)} %collective-permute-done.2, ...), kind=kOutput, calls=%fused_computation.27 | convolution fusion | flops 27804032 | bytes 1702912 | tf_op jit(solution)/shard_map/kyx,vkz->vzyx/dot_general | solution.py:52
  85.2 3.8 %collective-permute-done.4 = f32[2,8,32,15]{3,2,1,0:T(8,128)S(1)} collective-permute-done((f32[2,8,32,15]{3,2,1,0:T(8,128)S(1)}, f32[2,8,32,15]{3,2,1,0:T(8,128)S(1)}, u32[]{:S(2)}, u32[]{:S(2)}) %collective-permute-start.4) | collective-permute-done | bytes 30752 | tf_op jit(solution)/shard_map/ppermute | solution.py:27
  89.0 3.8 %collective-permute-done.5 = f32[2,8,32,15]{3,2,1,0:T(8,128)S(1)} collective-permute-done((f32[2,8,32,15]{3,2,1,0:T(8,128)S(1)}, f32[2,8,32,15]{3,2,1,0:T(8,128)S(1)}, u32[]{:S(2)}, u32[]{:S(2)}) %collective-permute-start.5) | collective-permute-done | bytes 30752 | tf_op jit(solution)/shard_map/ppermute | solution.py:29
  94.2 4.7 %collective-permute-start.6 = (f32[2,8,15,286]{3,2,1,0:T(8,128)}, f32[2,8,15,286]{3,2,1,0:T(8,128)}, u32[]{:S(2)}, u32[]{:S(2)}) collective-permute-start(f32[2,8,15,286]{3,2,1,0:T(8,128)} %get-tuple-element.10), channel_id=1, source_target_pairs={{0,1},{1,2},{2,3},{3,4},{4,5},{5,6},{6,7},{7,8},{8,9},{9,10},{10,1... | collective-permute-start | bytes 823688 | tf_op jit(solution)/shard_map/ppermute | solution.py:27
  102.9 5.6 %gather_fusion = f32[1984,2]{1,0:T(8,128)S(1)} fusion(f32[2,31]{0,1:T(8,128)S(1)} %copy.92, s32[2048]{0:T(1024)S(1)} %pad_clamp_fusion.1), kind=kCustom, calls=%fused_computation.clone | custom fusion | bytes 39680 | tf_op jit(solution)/shard_map/vmap(jit(_take))/gather | solution.py:42
  109.7 37.8 %gather_fusion.5 = f32[20224,2]{1,0:T(8,128)} fusion(f32[2,31]{0,1:T(8,128)S(1)} %copy.108, s32[20480]{0:T(1024)S(1)} %pad_clamp_fusion), kind=kCustom, calls=%fused_computation.5.clone | custom fusion | bytes 404480 | tf_op jit(solution)/shard_map/vmap(jit(_take))/gather | solution.py:42
  147.5 6.0 %copy.109 = f32[158,128,2]{1,0,2:T(8,128)S(1)} copy(f32[158,128,2]{2,1,0:T(8,128)} %bitcast.148) | data formatting | bytes 323584 | tf_op jit(solution)/shard_map/vmap(jit(_take))/gather | solution.py:42
  163.9 3.8 %collective-permute-done.9 = f32[8,32,15]{2,0,1:T(8,128)S(1)} collective-permute-done((f32[8,32,15]{2,0,1:T(8,128)S(1)}, f32[8,32,15]{2,0,1:T(8,128)S(1)}, u32[]{:S(2)}, u32[]{:S(2)}) %collective-permute-start.9) | collective-permute-done | bytes 15392 | tf_op jit(solution)/shard_map/ppermute | solution.py:29
  167.9 5.4 %collective-permute-start.10 = (f32[8,15,286]{2,0,1:T(8,128)S(1)}, f32[8,15,286]{2,0,1:T(8,128)S(1)}, u32[]{:S(2)}, u32[]{:S(2)}) collective-permute-start(f32[8,15,286]{2,0,1:T(8,128)S(1)} %get-tuple-element.14), channel_id=1, source_target_pairs={{0,1},{1,2},{2,3},{3,4},{4,5},{5,6},{6,7},{7,8},{8,9},{9,10},{10,1... | collective-permute-start | bytes 411848 | tf_op jit(solution)/shard_map/ppermute | solution.py:27
  175.8 5.3 %collective-permute-done.11 = f32[8,15,286]{2,0,1:T(8,128)S(1)} collective-permute-done((f32[8,15,286]{2,0,1:T(8,128)S(1)}, f32[8,15,286]{2,0,1:T(8,128)S(1)}, u32[]{:S(2)}, u32[]{:S(2)}) %collective-permute-start.11) | collective-permute-done | bytes 137312 | tf_op jit(solution)/shard_map/ppermute | solution.py:29
  187.7 2.2 collective-permute-done.12
  189.9 4.1 %collective-permute-done.13 = f32[2,8,32,15]{3,2,1,0:T(8,128)S(1)} collective-permute-done((f32[2,8,32,15]{3,2,1,0:T(8,128)S(1)}, f32[2,8,32,15]{3,2,1,0:T(8,128)S(1)}, u32[]{:S(2)}, u32[]{:S(2)}) %collective-permute-start.13) | collective-permute-done | bytes 30752 | tf_op jit(solution)/shard_map/ppermute | solution.py:29
  194.5 4.3 %collective-permute-start.14 = (f32[2,8,15,286]{3,2,1,0:T(8,128)S(1)}, f32[2,8,15,286]{3,2,1,0:T(8,128)S(1)}, u32[]{:S(2)}, u32[]{:S(2)}) collective-permute-start(f32[2,8,15,286]{3,2,1,0:T(8,128)S(1)} %get-tuple-element.6), channel_id=1, source_target_pairs={{0,1},{1,2},{2,3},{3,4},{4,5},{5,6},{6,7},{7,8},{8,9},{9,10},{10,1... | collective-permute-start | bytes 823688 | tf_op jit(solution)/shard_map/ppermute | solution.py:27
  198.7 2.1 collective-permute-start.15
  200.9 2.6 %collective-permute-done.14 = f32[2,8,15,286]{3,2,1,0:T(8,128)S(1)} collective-permute-done((f32[2,8,15,286]{3,2,1,0:T(8,128)S(1)}, f32[2,8,15,286]{3,2,1,0:T(8,128)S(1)}, u32[]{:S(2)}, u32[]{:S(2)}) %collective-permute-start.14) | collective-permute-done | bytes 274592 | tf_op jit(solution)/shard_map/ppermute | solution.py:27
  203.5 5.3 %collective-permute-done.15 = f32[2,8,15,286]{3,2,1,0:T(8,128)S(1)} collective-permute-done((f32[2,8,15,286]{3,2,1,0:T(8,128)S(1)}, f32[2,8,15,286]{3,2,1,0:T(8,128)S(1)}, u32[]{:S(2)}, u32[]{:S(2)}) %collective-permute-start.15) | collective-permute-done | bytes 274592 | tf_op jit(solution)/shard_map/ppermute | solution.py:29
  214.0 8.6 %all_gather.7 = f32[8,32,512]{2,0,1:T(8,128)S(1)} all-gather(f32[8,32,256]{2,0,1:T(8,128)S(1)} %fusion.61), channel_id=1, replica_groups=mesh['view'=2,'tile'=16] {'view'}, dimensions={2}, use_global_device_ids=true | all-gather | bytes 786432 | tf_op jit(solution)/shard_map/all_gather | solution.py:89
  (114 shorter events, 46.6 us)
Async XLA Ops:
  0.0 5.8 %copy-start.3 = (f32[1,8,32,512]{3,2,1,0:T(8,128)S(1)}, f32[1,8,32,512]{3,2,1,0:T(8,128)}, u32[]{:S(2)}) copy-start(f32[1,8,32,512]{3,2,1,0:T(8,128)} %param.10) | copy-start | bytes 1572868
  1.3 17.2 %collective-permute-start = (f32[8,32,15]{2,0,1:T(8,128)S(1)}, f32[8,32,15]{2,0,1:T(8,128)S(1)}, u32[]{:S(2)}, u32[]{:S(2)}) collective-permute-start(f32[8,32,15]{2,0,1:T(8,128)S(1)} %get-tuple-element.24), channel_id=1, source_target_pairs={{0,16},{1,17},{2,18},{3,19},{4,20},{5,21},{6,22},{7,23},{8,24},{9,... | collective-permute-start | bytes 46088 | tf_op jit(solution)/shard_map/ppermute | solution.py:27
  4.5 5.8 %copy-start.12 = (f32[1,3,31]{2,0,1:T(1,128)S(1)}, f32[1,3,31]{2,0,1:T(1,128)}, u32[]{:S(2)}) copy-start(f32[1,3,31]{2,0,1:T(1,128)} %param.11) | copy-start | bytes 1120
  4.5 14.0 %collective-permute-start.1 = (f32[8,32,15]{2,0,1:T(8,128)S(1)}, f32[8,32,15]{2,0,1:T(8,128)S(1)}, u32[]{:S(2)}, u32[]{:S(2)}) collective-permute-start(f32[8,32,15]{2,0,1:T(8,128)S(1)} %get-tuple-element.25), channel_id=1, source_target_pairs={{16,0},{17,1},{18,2},{19,3},{20,4},{21,5},{22,6},{23,7},{24,8},{25... | collective-permute-start | bytes 46088 | tf_op jit(solution)/shard_map/ppermute | solution.py:29
  6.7 75.5 %all-to-all-start = ((f32[2,1,8,32,256]{4,3,2,1,0:T(8,128)}), f32[2,1,8,32,256]{4,3,2,1,0:T(8,128)S(1)}, u32[]{:S(2)}, u32[]{:S(2)}) async-start(f32[2,1,8,32,256]{4,3,2,1,0:T(8,128)} %pad_maximum_fusion.4), calls=%async_computation | async-start | bytes 1048576 | tf_op jit(solution)/shard_map/all_to_all | solution.py:14
  19.4 58.0 %collective-permute-start.2 = (f32[8,15,286]{2,0,1:T(8,128)}, f32[8,15,286]{2,0,1:T(8,128)}, u32[]{:S(2)}, u32[]{:S(2)}) collective-permute-start(f32[8,15,286]{2,0,1:T(8,128)} %get-tuple-element.20), channel_id=1, source_target_pairs={{0,1},{1,2},{2,3},{3,4},{4,5},{5,6},{6,7},{7,8},{8,9},{9,10},{10,1... | collective-permute-start | bytes 411848 | tf_op jit(solution)/shard_map/ppermute | solution.py:27
  24.3 53.1 %collective-permute-start.3 = (f32[8,15,286]{2,0,1:T(8,128)S(1)}, f32[8,15,286]{2,0,1:T(8,128)}, u32[]{:S(2)}, u32[]{:S(2)}) collective-permute-start(f32[8,15,286]{2,0,1:T(8,128)S(1)} %get-tuple-element.21), channel_id=1, source_target_pairs={{1,0},{2,1},{3,2},{4,3},{5,4},{6,5},{7,6},{8,7},{9,8},{10,9},{11,1... | collective-permute-start | bytes 411848 | tf_op jit(solution)/shard_map/ppermute | solution.py:29
  26.3 51.2 %copy-start.8 = (pred[8,8]{1,0:T(8,128)(4,1)}, pred[8,8]{1,0:T(8,128)(4,1)S(1)}, u32[]{:S(2)}) copy-start(pred[8,8]{1,0:T(8,128)(4,1)S(1)} %get-tuple-element.29) | copy-start | bytes 196
  26.3 51.2 %copy-start.10 = (pred[8,8]{1,0:T(8,128)(4,1)}, pred[8,8]{1,0:T(8,128)(4,1)S(1)}, u32[]{:S(2)}) copy-start(pred[8,8]{1,0:T(8,128)(4,1)S(1)} %get-tuple-element.30) | copy-start | bytes 196
  27.2 50.2 %copy-start.5 = (f32[8,8,2]{1,0,2:T(8,128)}, f32[8,8,2]{1,0,2:T(8,128)S(1)}, u32[]{:S(2)}) copy-start(f32[8,8,2]{1,0,2:T(8,128)S(1)} %copy.129) | copy-start | bytes 1540
  82.5 6.5 %collective-permute-start.4 = (f32[2,8,32,15]{3,2,1,0:T(8,128)S(1)}, f32[2,8,32,15]{3,2,1,0:T(8,128)S(1)}, u32[]{:S(2)}, u32[]{:S(2)}) collective-permute-start(f32[2,8,32,15]{3,2,1,0:T(8,128)S(1)} %get-tuple-element.16), channel_id=1, source_target_pairs={{0,16},{1,17},{2,18},{3,19},{4,20},{5,21},{6,22},{7,23},{8,24},{9,... | collective-permute-start | bytes 92168 | tf_op jit(solution)/shard_map/ppermute | solution.py:27
  83.9 8.9 %collective-permute-start.5 = (f32[2,8,32,15]{3,2,1,0:T(8,128)S(1)}, f32[2,8,32,15]{3,2,1,0:T(8,128)S(1)}, u32[]{:S(2)}, u32[]{:S(2)}) collective-permute-start(f32[2,8,32,15]{3,2,1,0:T(8,128)S(1)} %get-tuple-element.17), channel_id=1, source_target_pairs={{16,0},{17,1},{18,2},{19,3},{20,4},{21,5},{22,6},{23,7},{24,8},{25... | collective-permute-start | bytes 92168 | tf_op jit(solution)/shard_map/ppermute | solution.py:29
  94.2 59.4 %collective-permute-start.6 = (f32[2,8,15,286]{3,2,1,0:T(8,128)}, f32[2,8,15,286]{3,2,1,0:T(8,128)}, u32[]{:S(2)}, u32[]{:S(2)}) collective-permute-start(f32[2,8,15,286]{3,2,1,0:T(8,128)} %get-tuple-element.10), channel_id=1, source_target_pairs={{0,1},{1,2},{2,3},{3,4},{4,5},{5,6},{6,7},{7,8},{8,9},{9,10},{10,1... | collective-permute-start | bytes 823688 | tf_op jit(solution)/shard_map/ppermute | solution.py:27
  98.9 54.7 %collective-permute-start.7 = (f32[2,8,15,286]{3,2,1,0:T(8,128)}, f32[2,8,15,286]{3,2,1,0:T(8,128)}, u32[]{:S(2)}, u32[]{:S(2)}) collective-permute-start(f32[2,8,15,286]{3,2,1,0:T(8,128)} %get-tuple-element.11), channel_id=1, source_target_pairs={{1,0},{2,1},{3,2},{4,3},{5,4},{6,5},{7,6},{8,7},{9,8},{10,9},{11,1... | collective-permute-start | bytes 823688 | tf_op jit(solution)/shard_map/ppermute | solution.py:29
  147.5 6.0 %copy-start.2 = (f32[2,8,32,15]{3,2,1,0:T(8,128)S(1)}, f32[2,8,32,15]{3,2,1,0:T(8,128)}, u32[]{:S(2)}) copy-start(f32[2,8,32,15]{3,2,1,0:T(8,128)} %copy-done.1) | copy-start | bytes 92164
  159.7 21.4 %copy-start.6 = (f32[8,8,2]{1,0,2:T(8,128)S(1)}, f32[8,8,2]{1,0,2:T(8,128)}, u32[]{:S(2)}) copy-start(f32[8,8,2]{1,0,2:T(8,128)} %copy-done.5) | copy-start | bytes 1540
  160.2 3.6 %collective-permute-start.8 = (f32[8,32,15]{2,0,1:T(8,128)S(1)}, f32[8,32,15]{2,0,1:T(8,128)S(1)}, u32[]{:S(2)}, u32[]{:S(2)}) collective-permute-start(f32[8,32,15]{2,0,1:T(8,128)S(1)} %get-tuple-element.22), channel_id=1, source_target_pairs={{0,16},{1,17},{2,18},{3,19},{4,20},{5,21},{6,22},{7,23},{8,24},{9,... | collective-permute-start | bytes 46088 | tf_op jit(solution)/shard_map/ppermute | solution.py:27
  161.5 6.1 %collective-permute-start.9 = (f32[8,32,15]{2,0,1:T(8,128)S(1)}, f32[8,32,15]{2,0,1:T(8,128)S(1)}, u32[]{:S(2)}, u32[]{:S(2)}) collective-permute-start(f32[8,32,15]{2,0,1:T(8,128)S(1)} %get-tuple-element.23), channel_id=1, source_target_pairs={{16,0},{17,1},{18,2},{19,3},{20,4},{21,5},{22,6},{23,7},{24,8},{25... | collective-permute-start | bytes 46088 | tf_op jit(solution)/shard_map/ppermute | solution.py:29
  167.9 7.9 %collective-permute-start.10 = (f32[8,15,286]{2,0,1:T(8,128)S(1)}, f32[8,15,286]{2,0,1:T(8,128)S(1)}, u32[]{:S(2)}, u32[]{:S(2)}) collective-permute-start(f32[8,15,286]{2,0,1:T(8,128)S(1)} %get-tuple-element.14), channel_id=1, source_target_pairs={{0,1},{1,2},{2,3},{3,4},{4,5},{5,6},{6,7},{7,8},{8,9},{9,10},{10,1... | collective-permute-start | bytes 411848 | tf_op jit(solution)/shard_map/ppermute | solution.py:27
  173.3 7.8 %collective-permute-start.11 = (f32[8,15,286]{2,0,1:T(8,128)S(1)}, f32[8,15,286]{2,0,1:T(8,128)S(1)}, u32[]{:S(2)}, u32[]{:S(2)}) collective-permute-start(f32[8,15,286]{2,0,1:T(8,128)S(1)} %get-tuple-element.15), channel_id=1, source_target_pairs={{1,0},{2,1},{3,2},{4,3},{5,4},{6,5},{7,6},{8,7},{9,8},{10,9},{11,1... | collective-permute-start | bytes 411848 | tf_op jit(solution)/shard_map/ppermute | solution.py:29
  185.1 4.8 %collective-permute-start.12 = (f32[2,8,32,15]{3,2,1,0:T(8,128)S(1)}, f32[2,8,32,15]{3,2,1,0:T(8,128)S(1)}, u32[]{:S(2)}, u32[]{:S(2)}) collective-permute-start(f32[2,8,32,15]{3,2,1,0:T(8,128)S(1)} %get-tuple-element.12), channel_id=1, source_target_pairs={{0,16},{1,17},{2,18},{3,19},{4,20},{5,21},{6,22},{7,23},{8,24},{9,... | collective-permute-start | bytes 92168 | tf_op jit(solution)/shard_map/ppermute | solution.py:27
  186.4 7.6 %collective-permute-start.13 = (f32[2,8,32,15]{3,2,1,0:T(8,128)S(1)}, f32[2,8,32,15]{3,2,1,0:T(8,128)S(1)}, u32[]{:S(2)}, u32[]{:S(2)}) collective-permute-start(f32[2,8,32,15]{3,2,1,0:T(8,128)S(1)} %get-tuple-element.13), channel_id=1, source_target_pairs={{16,0},{17,1},{18,2},{19,3},{20,4},{21,5},{22,6},{23,7},{24,8},{25... | collective-permute-start | bytes 92168 | tf_op jit(solution)/shard_map/ppermute | solution.py:29
  194.5 9.0 %collective-permute-start.14 = (f32[2,8,15,286]{3,2,1,0:T(8,128)S(1)}, f32[2,8,15,286]{3,2,1,0:T(8,128)S(1)}, u32[]{:S(2)}, u32[]{:S(2)}) collective-permute-start(f32[2,8,15,286]{3,2,1,0:T(8,128)S(1)} %get-tuple-element.6), channel_id=1, source_target_pairs={{0,1},{1,2},{2,3},{3,4},{4,5},{5,6},{6,7},{7,8},{8,9},{9,10},{10,1... | collective-permute-start | bytes 823688 | tf_op jit(solution)/shard_map/ppermute | solution.py:27
  198.7 10.0 %collective-permute-start.15 = (f32[2,8,15,286]{3,2,1,0:T(8,128)S(1)}, f32[2,8,15,286]{3,2,1,0:T(8,128)S(1)}, u32[]{:S(2)}, u32[]{:S(2)}) collective-permute-start(f32[2,8,15,286]{3,2,1,0:T(8,128)S(1)} %get-tuple-element.8), channel_id=1, source_target_pairs={{1,0},{2,1},{3,2},{4,3},{5,4},{6,5},{7,6},{8,7},{9,8},{10,9},{11,1... | collective-permute-start | bytes 823688 | tf_op jit(solution)/shard_map/ppermute | solution.py:29
  (6 other events, 9.4 us)
